TPU v7x, 256 devices: a whole 4x4x8 slice. The times are simulated.
256 devices in a mesh: roll: 64 (over z, y_lo, x), tp: 4 (over y_hi, core).
Axes of the slice: x: 4, y: 4 (y_hi: 2, y_lo: 2; y = y_hi * 2 + y_lo), z: 8, core: 2. Of those that a mesh axis runs over, the one named last changes fastest.
Arguments:
- hidden_in: bfloat16 [8192, 5120], P('roll', 'tp'), may hold values from -480 to 480
- qkv_weight: bfloat16 [5120, 3584], P('roll', 'tp'), may hold values from -1 to 1
- sample_group: int32 [8192], P('roll'), may hold values from 0 to 127, as said below
- prefix_blocks: int32 [128], P('roll'), may hold values from 1 to 4, as said below
- prefix_kv: bfloat16 [128, 512, 1024], P('roll', None, 'tp'), may hold values from -24 to 24
- page_table: int32 [8192, 2], P('roll'), may hold values from 0 to 255, as said below
- suffix_pool: bfloat16 [16384, 16, 1024], P('roll', None, 'tp'), may hold values from -24 to 24
Outputs:
- attended: bfloat16 [8192, 2560], P('roll', 'tp')
Inputs may be any that keep to these rules, and one draw needn't show every extreme that they name: `sample_group`: on each index of roll the 128 entries name every group exactly once. `prefix_blocks`: some group has exactly 4 blocks. `page_table`: on each index of roll the entries are a permutation of 0 to 255.
All inputs are finite; a program needn't handle non-finite values.
Results may differ from a plain program's by a relative error of at most 0.0096.
Values may be sent and summed in bfloat16 or wider, within the bound.
A program may use at most 64 MiB of HBM per device.

v0:
```python
import math
import jax
import jax.numpy as jnp
from jax import lax
from jax.sharding import PartitionSpec as P

HEADS = 20
KV_HEADS = 4
HD = 128
BLOCK = 128
PAGE = 16
SPAGES = 2
MASKED = -1e30


def softmax_parts(scores):
    row_max = jnp.max(scores, axis=-1)
    exponent = jnp.exp(scores - row_max[..., None])
    row_sum = jnp.sum(exponent, axis=-1)
    return (exponent, row_max, row_sum)


def merge_parts(first_out, first_lse, second_out, second_lse):
    combined = jnp.logaddexp(first_lse, second_lse)
    mixed = (
        jnp.exp(first_lse - combined)[..., None] * first_out
        + jnp.exp(second_lse - combined)[..., None] * second_out
    )
    return mixed.astype(jnp.bfloat16)


def per_device(
    hidden_in, qkv_weight, sample_group, prefix_blocks, prefix_kv, page_table, suffix_pool
):
    whole = lax.all_gather(hidden_in, "tp", axis=1, tiled=True)
    row_count = whole.shape[0]
    kv_heads_dev = prefix_kv.shape[2] // (2 * HD)
    repeat = HEADS // KV_HEADS
    q_width = kv_heads_dev * repeat * HD
    head_count = kv_heads_dev * repeat
    owned_groups = prefix_kv.shape[0]
    roll_count = lax.axis_size("roll")
    per_group = row_count // (roll_count * owned_groups)
    owner_rows = roll_count * per_group
    prefix_span = prefix_kv.shape[1]
    score_scale = 1.0 / math.sqrt(HD)
    float_in = whole.astype(jnp.float32)
    normed = (
        float_in * lax.rsqrt(jnp.mean(float_in * float_in, axis=-1, keepdims=True) + 1e-06)
    ).astype(jnp.bfloat16)
    united_proj = jnp.dot(
        normed,
        lax.all_gather(qkv_weight, "roll", axis=0, tiled=True),
        preferred_element_type=jnp.float32,
    )
    united_proj = united_proj.astype(jnp.bfloat16).reshape(row_count, kv_heads_dev, repeat + 2, HD)
    queries = united_proj[:, :, :repeat]
    own_key = united_proj[:, :, repeat]
    own_value = united_proj[:, :, repeat + 1]
    sort_order = jnp.argsort(sample_group, stable=True)

    def sample_layout(arrived, width, dtype):
        return (
            jnp.zeros((row_count, width), dtype)
            .at[sort_order]
            .set(arrived.reshape(row_count, width))
        )

    page_rows = suffix_pool[page_table].reshape(row_count, SPAGES * PAGE, kv_heads_dev, 2, HD)
    key_rows = jnp.concatenate([page_rows[:, :, :, 0], own_key[:, None]], axis=1)
    value_rows = jnp.concatenate([page_rows[:, :, :, 1], own_value[:, None]], axis=1)
    scores = (
        jnp.einsum("sjrd,stjd->sjrt", queries, key_rows, preferred_element_type=jnp.float32)
        * score_scale
    )
    exponent, row_max, row_sum = softmax_parts(scores)
    weights = (exponent / row_sum[..., None]).astype(jnp.bfloat16)
    result = jnp.einsum("sjrt,stjd->sjrd", weights, value_rows, preferred_element_type=jnp.float32)
    local_out = result
    local_lse = row_max + jnp.log(row_sum)
    incoming = lax.all_to_all(
        queries.reshape(row_count, q_width)[sort_order].reshape(
            roll_count, owned_groups, per_group, q_width
        ),
        "roll",
        split_axis=0,
        concat_axis=2,
        tiled=True,
    )
    kv_cache = prefix_kv.reshape(owned_groups, prefix_span, kv_heads_dev, 2, HD)
    scores = (
        jnp.einsum(
            "gqjrd,gtjd->gqjrt",
            incoming.reshape(owned_groups, owner_rows, kv_heads_dev, repeat, HD),
            kv_cache[:, :, :, 0],
            preferred_element_type=jnp.float32,
        )
        * score_scale
    )
    live_mask = (jnp.arange(prefix_span)[None, :] < prefix_blocks[:, None] * BLOCK)[
        :, None, None, None, :
    ]
    scores = jnp.where(live_mask, scores, MASKED)
    row_max = jnp.max(scores, axis=-1)
    exponent = jnp.where(live_mask, jnp.exp(scores - row_max[..., None]), 0.0)
    row_sum = jnp.sum(exponent, axis=-1)
    weights = (exponent / row_sum[..., None]).astype(jnp.bfloat16)
    result = jnp.einsum(
        "gqjrt,gtjd->gqjrd", weights, kv_cache[:, :, :, 1], preferred_element_type=jnp.float32
    )
    result, result_lse = (result, row_max + jnp.log(row_sum))
    back_out = lax.all_to_all(
        result.reshape(1, owned_groups, owner_rows, q_width),
        "roll",
        split_axis=2,
        concat_axis=0,
        tiled=True,
    )
    back_lse = lax.all_to_all(
        result_lse.reshape(1, owned_groups, owner_rows, head_count),
        "roll",
        split_axis=2,
        concat_axis=0,
        tiled=True,
    )
    prefix_out = sample_layout(back_out, q_width, jnp.float32)
    prefix_lse = sample_layout(back_lse, head_count, jnp.float32)
    prefix_out, prefix_lse = (
        prefix_out.reshape(row_count, kv_heads_dev, repeat, HD),
        prefix_lse.reshape(row_count, kv_heads_dev, repeat),
    )
    return merge_parts(prefix_out, prefix_lse, local_out, local_lse).reshape(row_count, q_width)


def solution(mesh):
    in_specs = (
        P("roll", "tp"),
        P("roll", "tp"),
        P("roll"),
        P("roll"),
        P("roll", None, "tp"),
        P("roll", None),
        P("roll", None, "tp"),
    )
    out_specs = P("roll", "tp")
    return jax.shard_map(
        per_device, mesh=mesh, in_specs=in_specs, out_specs=out_specs, check_vma=False
    )
```

profile of v0, /device:TPU:16, one launch (start us, length us, event | category | flops | bytes accessed | tf_op | source)
XLA Modules:
  0.0 428.6 jit_solution(3843228985545048968)
XLA Ops:
  6.5 0.0 copy-start
  6.5 0.0 all-gather.3.cloned.1.call-start
  6.5 0.7 all-gather.3.cloned.1.call-update
  7.3 0.0 all-gather.5.cloned.1.call-start
  7.3 0.7 all-gather.5.cloned.1.call-update
  8.0 0.7 compare_select_fusion
  8.7 0.1 copy.141
  8.8 0.1 reshape.204
  8.9 2.0 copy.137
  11.0 0.0 copy-done
  11.0 2.1 gather_fusion.1
  13.1 4.0 reshape.185
  17.1 0.0 copy-done.5
  17.1 2.5 sort.17
  19.6 0.0 copy-done.6
  19.6 0.1 iota_compare_fusion
  19.7 7.5 %fusion.40 = (bf16[128,32,1,1,128]{4,3,1,0,2:T(2,128)(2,1)}, bf16[128,32,1,1,128]{4,3,1,0,2:T(2,128)(2,1)}) fusion(bf16[128,32,1,2,128]{4,3,1,0,2:T(2,128)(2,1)} %reshape.185), kind=kLoop, calls=%fused_computation.69 | loop fusion | bytes 4194304 | tf_op jit(solution)/shard_map/slice | solution.py:70
  27.2 6.8 %all-gather.3.cloned.1.call-done = bf16[128,5120]{1,0:T(8,128)(2,1)} async-done(((bf16[128,1280]{1,0:T(8,128)(2,1)}), bf16[128,5120]{1,0:T(8,128)(2,1)}) %all-gather.3.cloned.1.call-update) | async-done | bytes 1310736 | tf_op jit(solution)/shard_map/all_gather | solution.py:35
  34.1 1.8 fusion
  35.8 316.4 %all-gather.5.cloned.1.call-done = bf16[5120,896]{1,0:T(8,128)(2,1)} async-done(((bf16[80,896]{1,0:T(8,128)(2,1)}), bf16[5120,896]{1,0:T(8,128)(2,1)}) %all-gather.5.cloned.1.call-update) | async-done | bytes 9175056 | tf_op jit(solution)/shard_map/all_gather | solution.py:53
  352.2 0.0 copy-done.1
  352.2 5.9 %fusion.19 = bf16[128,896]{1,0:T(8,128)(2,1)} fusion(bf16[5120,896]{1,0:T(8,128)(2,1)} %all-gather.5.cloned.1.call-done, bf16[128,5120]{1,0:T(8,128)(2,1)S(1)} %copy-done.1, f32[128]{0:T(128)S(1)} %add_rsqrt_fusion), kind=kOutput, calls=%fused_computation.30 | convolution fusion | flops 1176485888 | bytes 10715648 | tf_op jit(solution)/shard_map/dot_general | solution.py:51
  358.1 1.1 copy.131
  359.2 0.0 copy-start.4
  359.2 0.0 copy-start.2
  359.2 0.2 copy.134
  359.4 0.9 gather_fusion
  360.3 0.7 reshape.179
  361.0 0.0 copy-done.4
  361.0 8.6 %all-to-all-start = ((bf16[64,2,1,640]{3,1,2,0:T(2,128)(2,1)}), bf16[64,2,1,640]{3,1,2,0:T(2,128)(2,1)S(1)}, u32[]{:S(2)}, u32[]{:S(2)}) async-start(bf16[64,2,1,640]{3,1,2,0:T(2,128)(2,1)} %bitcast.2), calls=%async_computation | async-start | bytes 327680 | tf_op jit(solution)/shard_map/all_to_all | solution.py:81
  369.6 4.1 copy_bitcast_fusion
  373.7 0.0 copy-done.2
  373.7 6.9 %all-to-all-done = bf16[64,2,1,640]{3,1,2,0:T(2,128)(2,1)S(1)} async-done(((bf16[64,2,1,640]{3,1,2,0:T(2,128)(2,1)}), bf16[64,2,1,640]{3,1,2,0:T(2,128)(2,1)S(1)}, u32[]{:S(2)}, u32[]{:S(2)}) %all-to-all-start) | async-done | bytes 163872 | tf_op jit(solution)/shard_map/all_to_all | solution.py:81
  380.6 0.8 reshape.234
  381.5 1.4 bitcast_reduce_fusion
  382.9 0.4 fusion.22
  383.3 0.7 copy.140
  384.1 4.6 %all-to-all-start.1 = ((f32[1,2,64,5]{3,1,0,2:T(2,128)}), f32[1,2,64,5]{3,1,0,2:T(2,128)S(1)}, u32[]{:S(2)}, u32[]{:S(2)}) async-start(f32[1,2,64,5]{3,1,0,2:T(2,128)} %copy.140), calls=%async_computation.1 | async-start | bytes 131072 | tf_op jit(solution)/shard_map/all_to_all | solution.py:119
  388.7 1.5 convolution_bitcast_fusion
  390.1 0.0 copy-start.3
  390.2 0.2 copy.165
  390.4 1.0 reshape.235
  391.3 7.9 %all-to-all-done.1 = f32[1,2,64,5]{3,1,0,2:T(2,128)S(1)} async-done(((f32[1,2,64,5]{3,1,0,2:T(2,128)}), f32[1,2,64,5]{3,1,0,2:T(2,128)S(1)}, u32[]{:S(2)}, u32[]{:S(2)}) %all-to-all-start.1) | async-done | bytes 2592 | tf_op jit(solution)/shard_map/all_to_all | solution.py:119
  399.3 4.6 %all-to-all-start.2 = ((f32[1,2,64,640]{3,1,0,2:T(2,128)}), f32[1,2,64,640]{3,1,0,2:T(2,128)S(1)}, u32[]{:S(2)}, u32[]{:S(2)}) async-start(f32[1,2,64,640]{3,1,0,2:T(2,128)} %reshape.235), calls=%async_computation.2 | async-start | bytes 655360 | tf_op jit(solution)/shard_map/all_to_all | solution.py:112
  403.9 0.8 fusion.41
  404.7 0.9 copy.167
  405.6 0.1 copy.170
  405.7 0.1 copy.173
  405.8 2.2 fusion.42
  408.0 0.1 copy.145
  408.1 0.4 fusion.25
  408.5 0.1 copy.144
  408.6 0.9 scatter_custom_fusion
  409.5 0.1 copy.149
  409.6 0.1 copy.150
  409.7 0.7 copy.156
  410.5 5.8 %all-to-all-done.2 = f32[1,2,64,640]{3,1,0,2:T(2,128)S(1)} async-done(((f32[1,2,64,640]{3,1,0,2:T(2,128)}), f32[1,2,64,640]{3,1,0,2:T(2,128)S(1)}, u32[]{:S(2)}, u32[]{:S(2)}) %all-to-all-start.2) | async-done | bytes 327712 | tf_op jit(solution)/shard_map/all_to_all | solution.py:112
  416.3 0.2 reshape.222
  416.5 1.1 scatter_custom_fusion.1
  417.6 0.2 copy.154
  417.7 1.0 copy.155
  418.8 2.0 fusion.18
  420.8 0.2 copy.159
  421.0 0.8 copy.160
  (13 shorter events, 0.1 us)
Async XLA Ops:
  6.5 4.5 %copy-start = (bf16[256,16,256]{2,1,0:T(8,128)(2,1)S(1)}, bf16[256,16,256]{2,1,0:T(8,128)(2,1)}, u32[]{:S(2)}) copy-start(bf16[256,16,256]{2,1,0:T(8,128)(2,1)} %param.13) | copy-start | bytes 6291460
  6.5 27.5 %all-gather.3.cloned.1.call-start = ((), (), s32[]{:S(2)}) async-start(), calls=%async_computation.3 | async-start | bytes 1638400 | tf_op jit(solution)/shard_map/all_gather | solution.py:35
  7.3 344.9 %all-gather.5.cloned.1.call-start = ((), (), s32[]{:S(2)}) async-start(), calls=%async_computation.4 | async-start | bytes 9318400 | tf_op jit(solution)/shard_map/all_gather | solution.py:53
  13.1 4.0 copy-start.5
  13.1 6.6 %copy-start.6 = (s32[2]{0:T(128)S(1)}, s32[2]{0:T(128)}, u32[]{:S(2)}) copy-start(s32[2]{0:T(128)} %param.10) | copy-start | bytes 28
  34.1 318.1 %copy-start.1 = (bf16[128,5120]{1,0:T(8,128)(2,1)S(1)}, bf16[128,5120]{1,0:T(8,128)(2,1)}, u32[]{:S(2)}) copy-start(bf16[128,5120]{1,0:T(8,128)(2,1)} %all-gather.3.cloned.1.call-done) | copy-start | bytes 3932164
  359.2 1.8 copy-start.4
  359.2 14.5 %copy-start.2 = (bf16[128,1,5,128]{0,3,2,1:T(8,128)(2,1)}, bf16[128,1,5,128]{0,3,2,1:T(8,128)(2,1)S(1)}, u32[]{:S(2)}) copy-start(bf16[128,1,5,128]{0,3,2,1:T(8,128)(2,1)S(1)} %slice.32) | copy-start | bytes 491524
  361.0 19.6 %all-to-all-start = ((bf16[64,2,1,640]{3,1,2,0:T(2,128)(2,1)}), bf16[64,2,1,640]{3,1,2,0:T(2,128)(2,1)S(1)}, u32[]{:S(2)}, u32[]{:S(2)}) async-start(bf16[64,2,1,640]{3,1,2,0:T(2,128)(2,1)} %bitcast.2), calls=%async_computation | async-start | bytes 327680 | tf_op jit(solution)/shard_map/all_to_all | solution.py:81
  384.1 15.2 %all-to-all-start.1 = ((f32[1,2,64,5]{3,1,0,2:T(2,128)}), f32[1,2,64,5]{3,1,0,2:T(2,128)S(1)}, u32[]{:S(2)}, u32[]{:S(2)}) async-start(f32[1,2,64,5]{3,1,0,2:T(2,128)} %copy.140), calls=%async_computation.1 | async-start | bytes 131072 | tf_op jit(solution)/shard_map/all_to_all | solution.py:119
  390.1 14.6 %copy-start.3 = (bf16[128,1,5,128]{0,3,2,1:T(8,128)(2,1)S(1)}, bf16[128,1,5,128]{0,3,2,1:T(8,128)(2,1)}, u32[]{:S(2)}) copy-start(bf16[128,1,5,128]{0,3,2,1:T(8,128)(2,1)} %copy-done.2) | copy-start | bytes 491524
  399.3 17.0 %all-to-all-start.2 = ((f32[1,2,64,640]{3,1,0,2:T(2,128)}), f32[1,2,64,640]{3,1,0,2:T(2,128)S(1)}, u32[]{:S(2)}, u32[]{:S(2)}) async-start(f32[1,2,64,640]{3,1,0,2:T(2,128)} %reshape.235), calls=%async_computation.2 | async-start | bytes 655360 | tf_op jit(solution)/shard_map/all_to_all | solution.py:112
Sparse Core Ops, SparseCore 0:
  9.2 24.8 all-gather.2
  35.9 316.2 all-gather.4
where the time goes:
time: 429 us
  waiting for transfers between devices  345 us (80%)
  local copies, waits for them, and re-layouts  33 us (8%)
  starting transfers between devices  17.9 us (4%)
  between operations  13.6 us (3%)
  matrix products  12.9 us (3%)
  other arithmetic  5.93 us (1%)
    all_gather x1, waiting for transfers between devices, per_device(): lax.all_gather(qkv_weight, 'roll', axis=0, tiled=True)  316 us
    all_to_all x1, starting transfers between devices, per_device(): lax.all_to_all(queries.reshape(row_count, q_width)[sort_order].reshape(ro...  8.61 us
  transfers between devices with their start and end apart: 5, of which 5 were waited for; matrix products, arithmetic and copies ran while one was open for 8% of the time, Pallas kernels for 0%

commit v1 on v0

--- a/solution.py
+++ b/solution.py
@@ -11,6 +11,13 @@
 PAGE = 16
 SPAGES = 2
 MASKED = -1e30
+
+
+def swapped_in(x, name, dim):
+    size = lax.axis_size(name)
+    blocks = jnp.stack([x for _ in range(size)])
+    blocks = lax.all_to_all(blocks, name, split_axis=0, concat_axis=0)
+    return jnp.concatenate(blocks, axis=dim)
 
 
 def softmax_parts(scores):
@@ -49,9 +56,7 @@
         float_in * lax.rsqrt(jnp.mean(float_in * float_in, axis=-1, keepdims=True) + 1e-06)
     ).astype(jnp.bfloat16)
     united_proj = jnp.dot(
-        normed,
-        lax.all_gather(qkv_weight, "roll", axis=0, tiled=True),
-        preferred_element_type=jnp.float32,
+        normed, swapped_in(qkv_weight, "roll", 0), preferred_element_type=jnp.float32
     )
     united_proj = united_proj.astype(jnp.bfloat16).reshape(row_count, kv_heads_dev, repeat + 2, HD)
     queries = united_proj[:, :, :repeat]

time: 429 us -> 302 us (0.70)
  waiting for transfers between devices: 345 us -> 203 us
  starting transfers between devices: 17.9 us -> 29.3 us
  local copies, waits for them, and re-layouts: 33 us -> 37.3 us
    all_gather x1 -> x0, waiting for transfers between devices: 316 us -> none  [per_device(): lax.all_gather(qkv_weight, 'roll', axis=0, tiled=True)]
    all_to_all x0 -> x1, waiting for transfers between devices: none -> 158 us  [swapped_in(): blocks = lax.all_to_all(blocks, name, split_axis=0, concat_axis=0)]
    all_gather x1, waiting for transfers between devices: 6.83 us -> 23.9 us  [per_device(): whole = lax.all_gather(hidden_in, 'tp', axis=1, tiled=True)]
    all_to_all x0 -> x1, starting transfers between devices: none -> 13 us  [swapped_in(): blocks = lax.all_to_all(blocks, name, split_axis=0, concat_axis=0)]
    another operation x1 -> x2, local copies, waits for them, and re-layouts: 0.84 us -> 6.12 us  [the longest x1 5.28 us: swapped_in(): blocks = jnp.stack([x for _ in range(size)])]
  transfers between devices with their start and end apart: 5 -> 5, of which waited for: 5 -> 5; matrix products, arithmetic and copies ran while one was open for 8% -> 11% of each run, Pallas kernels for 0% -> 0%
where the time goes in v1:
time: 302 us
  waiting for transfers between devices  203 us (67%)
  local copies, waits for them, and re-layouts  37.3 us (12%)
  starting transfers between devices  29.3 us (10%)
  between operations  13.6 us (5%)
  matrix products  12.9 us (4%)
  other arithmetic  5.25 us (2%)
    all_to_all x1, waiting for transfers between devices, swapped_in(): blocks = lax.all_to_all(blocks, name, split_axis=0, concat_axis=0)  158 us
    all_gather x1, waiting for transfers between devices, per_device(): whole = lax.all_gather(hidden_in, 'tp', axis=1, tiled=True)  23.9 us
    all_to_all x1, starting transfers between devices, swapped_in(): blocks = lax.all_to_all(blocks, name, split_axis=0, concat_axis=0)  13 us
    all_to_all x1, waiting for transfers between devices, per_device(): lax.all_to_all(result_lse.reshape(1, owned_groups, owner_rows, head_count...  7.95 us
    slice x1, local copies, waits for them, and re-layouts, per_device(): page_rows[:, :, :, 0]  7.48 us
    all_to_all x1, waiting for transfers between devices, per_device(): lax.all_to_all(queries.reshape(row_count, q_width)[sort_order].reshape(ro...  7.01 us
    all_to_all x1, starting transfers between devices, per_device(): lax.all_to_all(queries.reshape(row_count, q_width)[sort_order].reshape(ro...  6.86 us
  transfers between devices with their start and end apart: 5, of which 5 were waited for; matrix products, arithmetic and copies ran while one was open for 11% of the time, Pallas kernels for 0%

profile of v1, /device:TPU:16, one launch (start us, length us, event | category | flops | bytes accessed | tf_op | source)
XLA Modules:
  0.0 301.6 jit_solution(840228505978401053)
XLA Ops:
  6.5 0.0 copy-start
  6.5 5.3 %stack.2 = bf16[64,80,896]{2,1,0:T(8,128)(2,1)} broadcast(bf16[80,896]{1,0:T(8,128)(2,1)} %param.8), dimensions={1,2} | broadcast | bytes 9318400 | tf_op jit(solution)/shard_map/stack | solution.py:18
  11.8 13.0 %all-to-all-start = ((bf16[64,80,896]{2,1,0:T(8,128)(2,1)}), bf16[64,80,896]{2,1,0:T(8,128)(2,1)}, u32[]{:S(2)}, u32[]{:S(2)}) async-start(bf16[64,80,896]{2,1,0:T(8,128)(2,1)} %stack.2), calls=%async_computation | async-start | bytes 18350080 | tf_op jit(solution)/shard_map/all_to_all | solution.py:19
  24.8 0.0 all-gather.2.cloned.1.call-start
  24.9 0.7 all-gather.2.cloned.1.call-update
  25.6 0.0 copy-done.6
  25.6 0.1 copy.141
  25.7 0.1 reshape.210
  25.9 0.0 copy-done
  25.9 2.1 gather_fusion.1
  28.0 4.0 %reshape.191 = bf16[128,32,1,2,128]{4,3,1,0,2:T(2,128)(2,1)} reshape(bf16[256,16,256]{2,1,0:T(8,128)(2,1)} %gather_fusion.1) | data formatting | bytes 4194304 | tf_op jit(solution)/shard_map/reshape | solution.py:74
  32.0 0.0 copy-done.5
  32.0 1.0 copy.137
  33.0 0.0 copy-done.7
  33.0 2.5 sort.17
  35.6 0.0 copy-done.8
  35.6 0.1 iota_compare_fusion
  35.7 7.5 %fusion.40 = (bf16[128,32,1,1,128]{4,3,1,0,2:T(2,128)(2,1)}, bf16[128,32,1,1,128]{4,3,1,0,2:T(2,128)(2,1)}) fusion(bf16[128,32,1,2,128]{4,3,1,0,2:T(2,128)(2,1)} %reshape.191), kind=kLoop, calls=%fused_computation.69 | loop fusion | bytes 4194304 | tf_op jit(solution)/shard_map/slice | solution.py:75
  43.1 23.9 %all-gather.2.cloned.1.call-done = bf16[128,5120]{1,0:T(8,128)(2,1)} async-done(((bf16[128,1280]{1,0:T(8,128)(2,1)}), bf16[128,5120]{1,0:T(8,128)(2,1)}) %all-gather.2.cloned.1.call-update) | async-done | bytes 1310736 | tf_op jit(solution)/shard_map/all_gather | solution.py:42
  67.1 1.8 fusion
  68.8 158.0 %all-to-all-done = bf16[64,80,896]{2,1,0:T(8,128)(2,1)} async-done(((bf16[64,80,896]{2,1,0:T(8,128)(2,1)}), bf16[64,80,896]{2,1,0:T(8,128)(2,1)}, u32[]{:S(2)}, u32[]{:S(2)}) %all-to-all-start) | async-done | bytes 9175072 | tf_op jit(solution)/shard_map/all_to_all | solution.py:19
  226.8 0.0 copy-done.1
  226.8 5.9 %fusion.19 = bf16[128,896]{1,0:T(8,128)(2,1)} fusion(bf16[5120,896]{1,0:T(8,128)(2,1)} %bitcast, bf16[128,5120]{1,0:T(8,128)(2,1)S(1)} %copy-done.1, f32[128]{0:T(128)S(1)} %add_rsqrt_fusion), kind=kOutput, calls=%fused_computation.30 | convolution fusion | flops 1176485888 | bytes 10715648 | tf_op jit(solution)/shard_map/dot_general | solution.py:58
  232.7 1.1 copy.131
  233.8 0.0 copy-start.4
  233.9 0.0 copy-start.2
  233.9 0.2 copy.134
  234.0 0.9 gather_fusion
  234.9 0.7 reshape.185
  235.7 0.0 copy-done.4
  235.7 6.9 %all-to-all-start.1 = ((bf16[64,2,1,640]{3,1,2,0:T(2,128)(2,1)}), bf16[64,2,1,640]{3,1,2,0:T(2,128)(2,1)S(1)}, u32[]{:S(2)}, u32[]{:S(2)}) async-start(bf16[64,2,1,640]{3,1,2,0:T(2,128)(2,1)} %bitcast.3), calls=%async_computation.1 | async-start | bytes 327680 | tf_op jit(solution)/shard_map/all_to_all | solution.py:86
  242.5 4.1 %copy_bitcast_fusion = (bf16[128,32,1,128]{3,1,0,2:T(8,128)(2,1)}, bf16[128,32,1,128]{3,1,0,2:T(8,128)(2,1)}) fusion(bf16[128,32,1,1,128]{4,3,1,0,2:T(2,128)(2,1)} %get-tuple-element.8, bf16[128,32,1,1,128]{4,3,1,0,2:T(2,128)(2,1)} %get-tuple-element.7), kind=kLoop, calls=%fused_computation.33 | loop fusion | bytes 4194304 | tf_op jit(solution)/shard_map/squeeze | solution.py:76
  246.6 0.0 copy-done.2
  246.6 7.0 %all-to-all-done.1 = bf16[64,2,1,640]{3,1,2,0:T(2,128)(2,1)S(1)} async-done(((bf16[64,2,1,640]{3,1,2,0:T(2,128)(2,1)}), bf16[64,2,1,640]{3,1,2,0:T(2,128)(2,1)S(1)}, u32[]{:S(2)}, u32[]{:S(2)}) %all-to-all-start.1) | async-done | bytes 163872 | tf_op jit(solution)/shard_map/all_to_all | solution.py:86
  253.6 0.8 reshape.240
  254.5 1.4 bitcast_reduce_fusion
  255.9 0.4 fusion.22
  256.3 0.7 copy.140
  257.1 4.6 %all-to-all-start.2 = ((f32[1,2,64,5]{3,1,0,2:T(2,128)}), f32[1,2,64,5]{3,1,0,2:T(2,128)S(1)}, u32[]{:S(2)}, u32[]{:S(2)}) async-start(f32[1,2,64,5]{3,1,0,2:T(2,128)} %copy.140), calls=%async_computation.2 | async-start | bytes 131072 | tf_op jit(solution)/shard_map/all_to_all | solution.py:124
  261.7 1.5 convolution_bitcast_fusion
  263.2 0.2 copy.165
  263.4 1.0 reshape.241
  264.3 7.9 %all-to-all-done.2 = f32[1,2,64,5]{3,1,0,2:T(2,128)S(1)} async-done(((f32[1,2,64,5]{3,1,0,2:T(2,128)}), f32[1,2,64,5]{3,1,0,2:T(2,128)S(1)}, u32[]{:S(2)}, u32[]{:S(2)}) %all-to-all-start.2) | async-done | bytes 2592 | tf_op jit(solution)/shard_map/all_to_all | solution.py:124
  272.3 4.8 %all-to-all-start.3 = ((f32[1,2,64,640]{3,1,0,2:T(2,128)}), f32[1,2,64,640]{3,1,0,2:T(2,128)S(1)}, u32[]{:S(2)}, u32[]{:S(2)}) async-start(f32[1,2,64,640]{3,1,0,2:T(2,128)} %reshape.241), calls=%async_computation.3 | async-start | bytes 655360 | tf_op jit(solution)/shard_map/all_to_all | solution.py:117
  277.1 0.8 fusion.41
  277.9 0.9 copy.167
  278.8 0.1 copy.173
  278.9 0.1 copy.170
  279.0 2.2 fusion.42
  281.2 0.1 copy.145
  281.3 0.4 fusion.25
  281.7 0.1 copy.144
  281.7 0.9 scatter_custom_fusion
  282.7 0.1 copy.149
  282.8 0.1 copy.156
  282.9 0.7 copy.150
  283.6 5.6 %all-to-all-done.3 = f32[1,2,64,640]{3,1,0,2:T(2,128)S(1)} async-done(((f32[1,2,64,640]{3,1,0,2:T(2,128)}), f32[1,2,64,640]{3,1,0,2:T(2,128)S(1)}, u32[]{:S(2)}, u32[]{:S(2)}) %all-to-all-start.3) | async-done | bytes 327712 | tf_op jit(solution)/shard_map/all_to_all | solution.py:117
  289.2 0.2 reshape.228
  289.5 1.1 scatter_custom_fusion.1
  290.6 0.2 copy.154
  290.7 1.0 copy.155
  291.8 2.0 fusion.18
  293.7 0.2 copy.159
  294.0 0.8 copy.160
  (17 shorter events, 0.1 us)
Async XLA Ops:
  6.5 19.3 %copy-start = (bf16[256,16,256]{2,1,0:T(8,128)(2,1)S(1)}, bf16[256,16,256]{2,1,0:T(8,128)(2,1)}, u32[]{:S(2)}) copy-start(bf16[256,16,256]{2,1,0:T(8,128)(2,1)} %param.13) | copy-start | bytes 6291460
  11.8 13.8 %copy-start.6 = (s32[128,2]{0,1:T(2,128)S(1)}, s32[128,2]{0,1:T(2,128)}, u32[]{:S(2)}) copy-start(s32[128,2]{0,1:T(2,128)} %param.12) | copy-start | bytes 3076
  11.8 215.0 %all-to-all-start = ((bf16[64,80,896]{2,1,0:T(8,128)(2,1)}), bf16[64,80,896]{2,1,0:T(8,128)(2,1)}, u32[]{:S(2)}, u32[]{:S(2)}) async-start(bf16[64,80,896]{2,1,0:T(8,128)(2,1)} %stack.2), calls=%async_computation | async-start | bytes 18350080 | tf_op jit(solution)/shard_map/all_to_all | solution.py:19
  24.8 42.2 %all-gather.2.cloned.1.call-start = ((), (), s32[]{:S(2)}) async-start(), calls=%async_computation.4 | async-start | bytes 1638400 | tf_op jit(solution)/shard_map/all_gather | solution.py:42
  28.0 4.0 %copy-start.5 = (bf16[2,512,256]{2,1,0:T(8,128)(2,1)S(1)}, bf16[2,512,256]{2,1,0:T(8,128)(2,1)}, u32[]{:S(2)}) copy-start(bf16[2,512,256]{2,1,0:T(8,128)(2,1)} %param.11) | copy-start | bytes 1572868
  28.0 5.1 %copy-start.7 = (s32[128]{0:T(128)S(1)}, s32[128]{0:T(128)}, u32[]{:S(2)}) copy-start(s32[128]{0:T(128)} %param.9) | copy-start | bytes 1540
  28.0 7.6 %copy-start.8 = (s32[2]{0:T(128)S(1)}, s32[2]{0:T(128)}, u32[]{:S(2)}) copy-start(s32[2]{0:T(128)} %param.10) | copy-start | bytes 28
  67.1 159.8 %copy-start.1 = (bf16[128,5120]{1,0:T(8,128)(2,1)S(1)}, bf16[128,5120]{1,0:T(8,128)(2,1)}, u32[]{:S(2)}) copy-start(bf16[128,5120]{1,0:T(8,128)(2,1)} %all-gather.2.cloned.1.call-done) | copy-start | bytes 3932164
  233.8 1.8 copy-start.4
  233.9 12.7 %copy-start.2 = (bf16[128,1,5,128]{0,3,2,1:T(8,128)(2,1)}, bf16[128,1,5,128]{0,3,2,1:T(8,128)(2,1)S(1)}, u32[]{:S(2)}) copy-start(bf16[128,1,5,128]{0,3,2,1:T(8,128)(2,1)S(1)} %slice.32) | copy-start | bytes 491524
  235.7 18.0 %all-to-all-start.1 = ((bf16[64,2,1,640]{3,1,2,0:T(2,128)(2,1)}), bf16[64,2,1,640]{3,1,2,0:T(2,128)(2,1)S(1)}, u32[]{:S(2)}, u32[]{:S(2)}) async-start(bf16[64,2,1,640]{3,1,2,0:T(2,128)(2,1)} %bitcast.3), calls=%async_computation.1 | async-start | bytes 327680 | tf_op jit(solution)/shard_map/all_to_all | solution.py:86
  257.1 15.2 %all-to-all-start.2 = ((f32[1,2,64,5]{3,1,0,2:T(2,128)}), f32[1,2,64,5]{3,1,0,2:T(2,128)S(1)}, u32[]{:S(2)}, u32[]{:S(2)}) async-start(f32[1,2,64,5]{3,1,0,2:T(2,128)} %copy.140), calls=%async_computation.2 | async-start | bytes 131072 | tf_op jit(solution)/shard_map/all_to_all | solution.py:124
  263.2 14.7 %copy-start.3 = (bf16[128,1,5,128]{0,3,2,1:T(8,128)(2,1)S(1)}, bf16[128,1,5,128]{0,3,2,1:T(8,128)(2,1)}, u32[]{:S(2)}) copy-start(bf16[128,1,5,128]{0,3,2,1:T(8,128)(2,1)} %copy-done.2) | copy-start | bytes 491524
  272.3 16.9 %all-to-all-start.3 = ((f32[1,2,64,640]{3,1,0,2:T(2,128)}), f32[1,2,64,640]{3,1,0,2:T(2,128)S(1)}, u32[]{:S(2)}, u32[]{:S(2)}) async-start(f32[1,2,64,640]{3,1,0,2:T(2,128)} %reshape.241), calls=%async_computation.3 | async-start | bytes 655360 | tf_op jit(solution)/shard_map/all_to_all | solution.py:117
Sparse Core Ops, SparseCore 0:
  27.5 39.5 all-gather.1
